TPU v7x, 32 devices: a whole 2x2x4 slice. The times are simulated.
32 devices in a mesh: ctx: 8 (over z, y), head: 4 (over x, core).
Axes of the slice: x: 2, y: 2, z: 4, core: 2. Of those that a mesh axis runs over, the one named last changes fastest.
Arguments:
- x_in: bfloat16 [4096, 8192], P('ctx', 'head'), may hold values from -6 to 6
- z_in: bfloat16 [4096, 8192], P('ctx', 'head'), may hold values from -6 to 6
- bc_in: bfloat16 [4096, 256], P('ctx', 'head'), may hold values from -6 to 6
- dt: float32 [4096, 128], P('ctx', 'head'), may hold values from 4.8828125e-05 to 0.25146484, as said below
- decay_scale: float32 [128], P('head'), may hold values from 0.5 to 2
- conv_x: bfloat16 [4, 8192], P(None, 'head'), may hold values from -3 to 3
- conv_bc: bfloat16 [4, 256], P(None, 'head'), may hold values from -3 to 3
- norm_gain: bfloat16 [8192], P('head'), may hold values from 0.25 to 1.75
- doc_start: int32 [4096], P('ctx'), may hold values from 0 to 1, as said below
Outputs:
- out: bfloat16 [4096, 8192], P('ctx', 'head')
Inputs may be any that keep to these rules, and one draw needn't show every extreme that they name: doc_start[0] = 0; going round the loop, two consecutive ones are at most 512 apart; the document that holds position 0 is exactly 512 long and begins 3 (4 - 1) or more positions before the end. `dt`: positive step sizes.
All inputs are finite; a program needn't handle non-finite values.
Results may differ from a plain program's by a relative error of at most 0.0034.
Values may be sent and summed in bfloat16 or wider, within the bound.
No kernel may reach another device: no remote copies, remote signals or barrier semaphores. Data moves between devices by JAX's collectives and lax.ppermute only.
A program may use at most 64 MiB of HBM per device.

v0:
```python
import jax
import jax.numpy as jnp
from jax import lax
from jax.sharding import PartitionSpec as P

HDIM = 64
DSTATE = 128
BLOCK = 256
CONV = 4


def shifted(value, axis, steps):
    count = lax.axis_size(axis)
    pairs = [(source, (source + steps) % count) for source in range(count)]
    return lax.ppermute(value, axis, pairs)


def causal_conv(padded, taps, same):
    rows = same.shape[1]
    total = jnp.zeros((rows, taps.shape[1]), jnp.float32)
    for offset in range(taps.shape[0]):
        piece = padded[offset : offset + rows].astype(jnp.float32) * taps[offset].astype(
            jnp.float32
        )
        total = total + jnp.where(same[offset][:, None], piece, 0.0)
    return jax.nn.silu(total)


def block_pass(state, values, bmat, cmat, steps, scale, doc_ids, doc_before):
    high = lax.Precision.HIGHEST
    log_decay = jnp.cumsum(-steps * scale[None, :], axis=0)
    scores = jnp.dot(cmat, bmat.T, precision=high)
    rows = doc_ids.shape[0]
    lower = jnp.arange(rows)[:, None] >= jnp.arange(rows)[None, :]
    keep = lower & (doc_ids[:, None] == doc_ids[None, :])
    decay_t = log_decay.T
    spread = decay_t[:, :, None] - decay_t[:, None, :]
    weights = (
        jnp.where(keep[None, :, :], jnp.exp(jnp.minimum(spread, 0.0)), 0.0) * scores[None, :, :]
    )
    output = jnp.einsum("hts,shp->htp", weights, values, precision=high)
    live = doc_ids == doc_before
    carried = jnp.einsum("tn,hpn->htp", cmat, state, precision=high)
    output = output + jnp.where(live[None, :, None], jnp.exp(decay_t)[:, :, None] * carried, 0.0)
    tail = doc_ids == doc_ids[-1]
    to_end = jnp.where(tail[:, None], jnp.exp(log_decay[-1][None, :] - log_decay), 0.0)
    fresh = jnp.einsum("sh,shp,sn->hpn", to_end, values, bmat, precision=high)
    keep_state = jnp.where(doc_ids[-1] == doc_before, jnp.exp(log_decay[-1]), 0.0)
    return (keep_state[:, None, None] * state + fresh, output)


def gated_norm(output, gate, gain):
    rows, heads, width = output.shape
    mixed = output * jax.nn.silu(gate.astype(jnp.float32)).reshape(rows, heads, width)
    factor = lax.rsqrt(jnp.mean(mixed * mixed, axis=-1, keepdims=True) + 1e-05)
    normed = mixed * factor * gain.astype(jnp.float32).reshape(heads, width)
    return normed.reshape(rows, heads * width).astype(jnp.bfloat16)


def on_device(x_in, z_in, bc_in, dt, decay_scale, conv_x, conv_bc, norm_gain, doc_start):
    high = lax.Precision.HIGHEST
    positions = x_in.shape[0]
    local_heads = dt.shape[1]
    lead = CONV - 1
    doc_ids = jnp.cumsum(doc_start)
    in_last = (doc_ids[-lead:] == doc_ids[-1])[:, None]
    tail_x = jnp.where(in_last, x_in[-lead:], jnp.zeros_like(x_in[-lead:]))
    tail_bc = jnp.where(in_last, bc_in[-lead:], jnp.zeros_like(bc_in[-lead:]))
    rim_x, rim_bc = shifted((tail_x, tail_bc), "ctx", 1)
    x_pad = jnp.concatenate([rim_x, x_in], axis=0)
    bc_pad = jnp.concatenate([rim_bc, bc_in], axis=0)
    ids_pad = jnp.concatenate([jnp.zeros((lead,), jnp.int32), doc_ids], axis=0)
    same = jnp.stack([ids_pad[offset : offset + positions] == doc_ids for offset in range(CONV)])
    x_conv = causal_conv(x_pad, conv_x, same)
    bc_local = causal_conv(bc_pad, conv_bc, same).astype(jnp.bfloat16)
    bc_whole = lax.all_gather(bc_local, "head", axis=1, tiled=True).astype(jnp.float32)
    bmat = bc_whole[:, :DSTATE]
    cmat = bc_whole[:, DSTATE:]
    blocks = positions // BLOCK
    empty = jnp.zeros((local_heads, HDIM, DSTATE), jnp.float32)
    end_state = empty
    pieces = []
    for index in range(blocks):
        low = index * BLOCK
        high_end = low + BLOCK
        before = jnp.full((), -1, jnp.int32) if index == 0 else doc_ids[low - 1]
        block_values = x_conv[low:high_end].reshape(BLOCK, local_heads, HDIM)
        end_state, block_out = block_pass(
            end_state,
            block_values,
            bmat[low:high_end],
            cmat[low:high_end],
            dt[low:high_end],
            decay_scale,
            doc_ids[low:high_end],
            before,
        )
        pieces.append(block_out)
    output = jnp.concatenate(pieces, axis=1)
    device_decay = jnp.cumsum(-dt * decay_scale[None, :], axis=0)
    through = jnp.where(doc_ids[-1] == 0, jnp.exp(device_decay[-1]), 0.0)

    def relay_turn(turn, incoming):
        return shifted(through[:, None, None] * incoming + end_state, "ctx", 1)

    state_in = lax.fori_loop(0, lax.axis_size("ctx") // 8, relay_turn, empty)
    carried = jnp.einsum("tn,hpn->htp", cmat, state_in, precision=high)
    live = (doc_ids == 0)[None, :, None]
    output = output + jnp.where(live, jnp.exp(device_decay.T)[:, :, None] * carried, 0.0)
    return gated_norm(jnp.transpose(output, (1, 0, 2)), z_in, norm_gain)


def solution(mesh):
    in_specs = (
        P("ctx", "head"),
        P("ctx", "head"),
        P("ctx", "head"),
        P("ctx", "head"),
        P("head"),
        P(None, "head"),
        P(None, "head"),
        P("head"),
        P("ctx"),
    )
    out_specs = P("ctx", "head")
    return jax.shard_map(
        on_device, mesh=mesh, in_specs=in_specs, out_specs=out_specs, check_vma=False
    )
```

profile of v0, /device:TPU:0, one launch (start us, length us, event | category | flops | bytes accessed | tf_op | source)
XLA Modules:
  0.0 98.0 jit_solution(13949360632276049648)
XLA Ops:
  0.0 1.0 %reduce-window.29 = s32[4,128]{1,0:T(4,128)S(1)} reduce-window(s32[4,128]{1,0:T(4,128)} %bitcast.145, s32[]{:T(128)} %constant.12.clone.1), window={size=1x128 pad=0_0x127_0}, to_apply=%region_0.0 | reduce-window | flops 65024 | bytes 4100 | tf_op jit(solution)/shard_map/reduce-window
  3.1 0.8 slice_select_fusion.1
  3.9 3.0 %collective-permute-start = (bf16[3,64]{0,1:T(8,128)(2,1)S(1)}, bf16[3,64]{0,1:T(8,128)(2,1)S(1)}, u32[]{:S(2)}, u32[]{:S(2)}) collective-permute-start(bf16[3,64]{0,1:T(8,128)(2,1)S(1)} %slice_select_fusion.1), channel_id=1, source_target_pairs={{0,4},{4,8},{8,12},{12,16},{16,20},{20,24},{24,28},{28,0},{1,5},{5... | collective-permute-start | bytes 1160 | tf_op jit(solution)/shard_map/ppermute | solution.py:15
  6.9 0.8 slice_select_fusion
  7.7 1.6 %collective-permute-start.1 = (bf16[3,2048]{1,0:T(4,128)(2,1)S(1)}, bf16[3,2048]{1,0:T(4,128)(2,1)S(1)}, u32[]{:S(2)}, u32[]{:S(2)}) collective-permute-start(bf16[3,2048]{1,0:T(4,128)(2,1)S(1)} %slice_select_fusion), channel_id=1, source_target_pairs={{0,4},{4,8},{8,12},{12,16},{16,20},{20,24},{24,28},{28,0},{1,5},{5... | collective-permute-start | bytes 36872 | tf_op jit(solution)/shard_map/ppermute | solution.py:15
  10.6 0.8 fusion.50
  11.4 0.8 multiply_bitcast_fusion.1
  15.1 0.9 copy_bitcast_fusion
  18.1 1.1 %reduce-window.39 = f32[32,4,128]{2,0,1:T(8,128)S(1)} reduce-window(f32[32,4,128]{2,0,1:T(8,128)S(1)} %copy_bitcast_fusion, f32[]{:T(128)} %constant.13.clone.1), window={size=1x1x128 pad=0_0x0_0x127_0}, to_apply=%region_6.7 | reduce-window | flops 2080768 | bytes 131076 | tf_op jit(solution)/shard_map/reduce-window.6
  19.7 0.8 bitcast_convert_fusion.3
  21.7 2.5 %broadcast_compare_fusion.1 = (pred[256]{0:T(512)(128)(4,1)S(1)}, pred[256]{0:T(512)(128)(4,1)}, pred[256]{0:T(512)(128)(4,1)S(1)}, pred[256]{0:T(512)(128)(4,1)}) fusion(s32[]{:T(128)} %bitcast.27, s32[4,128]{1,0:T(4,128)S(1)} %get-tuple-element.16, s32[]{:T(128)} %bitcast.19, s32[]{:T(128)} %bitcast.20), kind=kLoop, calls=%fused_computation.127 | loop fusion | flops 1024 | bytes 3084 | tf_op jit(solution)/shard_map/eq | solution.py:45
  24.4 0.9 slice_convert_fusion.3
  27.4 4.7 %convert_multiply_fusion = f32[512,2048]{1,0:T(8,128)} fusion(bf16[512,2048]{1,0:T(8,128)(2,1)} %param.10), kind=kLoop, calls=%fused_computation.12 | loop fusion | flops 5242880 | bytes 6291456 | tf_op jit(solution)/shard_map/jit(silu)/mul | solution.py:54
  32.0 0.8 fusion.71
  32.8 5.5 %copy.68 = f32[512,2048]{0,1:T(8,128)} copy(f32[512,2048]{1,0:T(8,128)} %convert_multiply_fusion) | data formatting | bytes 8388608 | tf_op jit(solution)/shard_map/jit(silu)/mul | solution.py:54
  38.6 5.8 %all_gather.3 = bf16[512,256]{0,1:T(8,128)(2,1)S(1)} all-gather(bf16[512,64]{0,1:T(8,128)(2,1)S(1)} %multiply_convert_fusion.1), channel_id=1, replica_groups=mesh['ctx'=8,'head'=4] {'head'}, dimensions={1}, use_global_device_ids=true | all-gather | bytes 327680 | tf_op jit(solution)/shard_map/all_gather | solution.py:76
  44.4 0.9 fusion.59
  45.3 2.3 %fusion.48 = f32[32,64,256]{2,1,0:T(8,128)} fusion(bf16[512,256]{0,1:T(8,128)(2,1)S(1)} %all_gather.3), kind=kOutput, calls=%fused_computation.49 | convolution fusion | flops 805306368 | bytes 2162688 | tf_op jit(solution)/shard_map/tn,hpn->htp/dot_general | solution.py:43
  47.6 0.9 fusion.64
  48.5 4.2 %divide_multiply_fusion = f32[512,2048]{1,0:T(8,128)S(1)} fusion(bf16[512,2048]{1,0:T(8,128)(2,1)S(1)} %copy-done.3, bf16[3,2048]{1,0:T(4,128)(2,1)S(1)} %collective-permute-done.1, f32[2048]{0:T(1024)S(1)} %bitcast.143, f32[2048]{0:T(1024)S(1)} %bitcast.144, f32[2048]{0:T(1024)S(1)} %bitcast.142, f32[2048]{0:T(1024)S(1)} %bitcast.141, ...), kind=kLoop, calls=%fused_computation.25 | loop fusion | flops 28311552 | bytes 6338048 | tf_op jit(solution)/shard_map/jit(silu)/mul | solution.py:26
  52.7 2.3 %fusion.83 = (f32[256,2048]{1,0:T(8,128)}, f32[256,2048]{1,0:T(8,128)}) fusion(f32[512,2048]{1,0:T(8,128)S(1)} %divide_multiply_fusion), kind=kLoop, calls=%fused_computation.139 | loop fusion | bytes 8388608 | tf_op jit(solution)/shard_map/slice | solution.py:87
  55.0 1.9 %copy.59 = f32[256,2048]{0,1:T(8,128)S(1)} copy(f32[256,2048]{1,0:T(8,128)} %get-tuple-element.20) | data formatting | bytes 4194304 | tf_op jit(solution)/shard_map/slice | solution.py:87
  56.9 1.7 %fusion.37 = f32[32,64,128]{2,1,0:T(8,128)S(1)} fusion(f32[256,32,64]{0,2,1:T(8,128)S(1)} %bitcast.136, f32[256,32]{0,1:T(8,128)S(1)} %exponential_select_fusion.1, f32[32]{0:T(128)} %fusion.75, bf16[512,256]{0,1:T(8,128)(2,1)S(1)} %all_gather.3), kind=kOutput, calls=%fused_computation.44 | convolution fusion | flops 806092800 | bytes 3244160 | tf_op jit(solution)/shard_map/sh,shp,sn->hpn/dot_general | solution.py:47
  58.7 2.4 %fusion.55 = f32[32,64,256]{2,1,0:T(8,128)} fusion(f32[32,64,128]{2,1,0:T(8,128)S(1)} %fusion.37, bf16[512,256]{0,1:T(8,128)(2,1)S(1)} %all_gather.3), kind=kOutput, calls=%fused_computation.68 | convolution fusion | flops 805306368 | bytes 3211264 | tf_op jit(solution)/shard_map/tn,hpn->htp/dot_general | solution.py:43
  61.0 1.9 %copy.64 = f32[256,2048]{0,1:T(8,128)S(1)} copy(f32[256,2048]{1,0:T(8,128)} %get-tuple-element.18) | data formatting | bytes 4194304 | tf_op jit(solution)/shard_map/slice | solution.py:87
  63.0 1.1 %fusion.43 = f32[32,64,128]{2,1,0:T(8,128)S(1)} fusion(f32[256,32,64]{0,2,1:T(8,128)S(1)} %bitcast.134, f32[256,32]{0,1:T(8,128)S(1)} %exponential_select_fusion, f32[32,64,128]{2,1,0:T(8,128)S(1)} %fusion.37, f32[32]{0:T(128)S(1)} %copy-done.18, f32[32]{0:T(128)S(1)} %copy-done.17, bf16[512,256]{0,1:T(8,128)(2,1)S(1)} %all_gather.3), kind=kOutput, calls=%fused_computation.46 | convolution fusion | flops 806617088 | bytes 4293632 | tf_op jit(solution)/shard_map/sh,shp,sn->hpn/dot_general | solution.py:47
  64.2 1.8 %collective-permute-start.2 = (f32[32,64,128]{2,1,0:T(8,128)S(1)}, f32[32,64,128]{2,1,0:T(8,128)S(1)}, u32[]{:S(2)}, u32[]{:S(2)}) collective-permute-start(f32[32,64,128]{2,1,0:T(8,128)S(1)} %fusion.43), channel_id=1, source_target_pairs={{0,4},{4,8},{8,12},{12,16},{16,20},{20,24},{24,28},{28,0},{1,5},{5... | collective-permute-start | bytes 3145736 | tf_op jit(solution)/shard_map/while/body/eval_jaxpr/ppermute | solution.py:15
  66.0 10.0 %bitcast_add_fusion = f32[32,256,64]{1,2,0:T(8,128)S(1)} fusion(f32[32,64,256]{2,1,0:T(8,128)S(1)} %copy-done.5, f32[256,32,64]{0,2,1:T(8,128)S(1)} %bitcast.135, f32[256,256]{1,0:T(8,128)S(1)} %copy-done.7, f32[32,256]{1,0:T(8,128)S(1)} %copy-done.11, pred[256,256]{1,0:T(8,128)(4,1)S(1)} %copy-done.10, f32[32,256]{1,0:T(8,128)S(1)} %copy-done.13, ...), kind=kOutput, calls=%fused_computation.38 | convolution fusion | flops 1620574208 | bytes 6684928 | tf_op jit(solution)/shard_map/hts,shp->htp/dot_general | solution.py:41
  76.1 10.2 %bitcast_add_fusion.1 = f32[32,256,64]{1,2,0:T(8,128)S(1)} fusion(f32[32,64,256]{2,1,0:T(8,128)S(1)} %copy-done.4, f32[256,32,64]{0,2,1:T(8,128)S(1)} %bitcast.137, f32[256,256]{1,0:T(8,128)S(1)} %copy-done.6, f32[32,256]{1,0:T(8,128)S(1)} %copy-done.12, pred[256,256]{1,0:T(8,128)(4,1)S(1)} %copy-done.9, f32[32,256]{1,0:T(8,128)S(1)} %copy-done.14, ...), kind=kOutput, calls=%fused_computation.39 | convolution fusion | flops 1620574208 | bytes 6684928 | tf_op jit(solution)/shard_map/hts,shp->htp/dot_general | solution.py:41
  86.3 6.2 %collective-permute-done.2 = f32[32,64,128]{2,1,0:T(8,128)S(1)} collective-permute-done((f32[32,64,128]{2,1,0:T(8,128)S(1)}, f32[32,64,128]{2,1,0:T(8,128)S(1)}, u32[]{:S(2)}, u32[]{:S(2)}) %collective-permute-start.2) | collective-permute-done | bytes 1048608 | tf_op jit(solution)/shard_map/while/body/eval_jaxpr/ppermute | solution.py:15
  92.5 2.5 %multiply_reduce_fusion = (f32[512,32]{0,1:T(8,128)S(1)}, f32[512,32,64]{0,2,1:T(8,128)S(1)}) fusion(f32[512,32,64]{0,2,1:T(8,128)S(1)} %bitcast.132, f32[32,64,128]{2,1,0:T(8,128)S(1)} %collective-permute-done.2, bf16[512,256]{0,1:T(8,128)(2,1)S(1)} %all_gather.3, f32[32,512]{1,0:T(8,128)S(1)} %bitcast_exponential_fusion, ...), kind=kOutput, calls=%fused_computation.21 | convolution fusion | flops 1617936384 | bytes 13894144 | tf_op jit(solution)/shard_map/tn,hpn->htp/dot_general | solution.py:107
  95.6 2.4 %copy.69 = bf16[512,2048]{1,0:T(8,128)(2,1)} copy(bf16[512,2048]{0,1:T(8,128)(2,1)S(1)} %bitcast.133) | data formatting | bytes 4194304 | tf_op jit(solution)/shard_map/convert_element_type | solution.py:57
  (82 shorter events, 10.6 us)
Async XLA Ops:
  3.9 34.5 %collective-permute-start = (bf16[3,64]{0,1:T(8,128)(2,1)S(1)}, bf16[3,64]{0,1:T(8,128)(2,1)S(1)}, u32[]{:S(2)}, u32[]{:S(2)}) collective-permute-start(bf16[3,64]{0,1:T(8,128)(2,1)S(1)} %slice_select_fusion.1), channel_id=1, source_target_pairs={{0,4},{4,8},{8,12},{12,16},{16,20},{20,24},{24,28},{28,0},{1,5},{5... | collective-permute-start | bytes 1160 | tf_op jit(solution)/shard_map/ppermute | solution.py:15
  7.7 40.8 %collective-permute-start.1 = (bf16[3,2048]{1,0:T(4,128)(2,1)S(1)}, bf16[3,2048]{1,0:T(4,128)(2,1)S(1)}, u32[]{:S(2)}, u32[]{:S(2)}) collective-permute-start(bf16[3,2048]{1,0:T(4,128)(2,1)S(1)} %slice_select_fusion), channel_id=1, source_target_pairs={{0,4},{4,8},{8,12},{12,16},{16,20},{20,24},{24,28},{28,0},{1,5},{5... | collective-permute-start | bytes 36872 | tf_op jit(solution)/shard_map/ppermute | solution.py:15
  32.8 5.5 %copy-start.15 = (bf16[2048]{0:T(1024)(128)(2,1)S(1)}, bf16[2048]{0:T(1024)(128)(2,1)}, u32[]{:S(2)}) copy-start(bf16[2048]{0:T(1024)(128)(2,1)} %param.16) | copy-start | bytes 12292
  32.8 5.6 %copy-start.8 = (bf16[512,64]{0,1:T(8,128)(2,1)S(1)}, bf16[512,64]{0,1:T(8,128)(2,1)}, u32[]{:S(2)}) copy-start(bf16[512,64]{0,1:T(8,128)(2,1)} %param.11) | copy-start | bytes 196612
  32.8 15.7 %copy-start.3 = (bf16[512,2048]{1,0:T(8,128)(2,1)S(1)}, bf16[512,2048]{1,0:T(8,128)(2,1)}, u32[]{:S(2)}) copy-start(bf16[512,2048]{1,0:T(8,128)(2,1)} %param.9) | copy-start | bytes 6291460
  56.9 4.1 %copy-start.1 = (f32[256,2048]{0,1:T(8,128)}, f32[256,2048]{0,1:T(8,128)S(1)}, u32[]{:S(2)}) copy-start(f32[256,2048]{0,1:T(8,128)S(1)} %copy.59) | copy-start | bytes 6291460
  58.6 4.4 %copy-start.17 = (f32[32]{0:T(128)S(1)}, f32[32]{0:T(128)}, u32[]{:S(2)}) copy-start(f32[32]{0:T(128)} %fusion.71) | copy-start | bytes 388
  58.7 4.4 %copy-start.18 = (f32[32]{0:T(128)S(1)}, f32[32]{0:T(128)}, u32[]{:S(2)}) copy-start(f32[32]{0:T(128)} %broadcast_select_fusion) | copy-start | bytes 388
  63.0 3.0 %copy-start.5 = (f32[32,64,256]{2,1,0:T(8,128)S(1)}, f32[32,64,256]{2,1,0:T(8,128)}, u32[]{:S(2)}) copy-start(f32[32,64,256]{2,1,0:T(8,128)} %fusion.55) | copy-start | bytes 6291460
  63.0 3.0 %copy-start.7 = (f32[256,256]{1,0:T(8,128)S(1)}, f32[256,256]{1,0:T(8,128)}, u32[]{:S(2)}) copy-start(f32[256,256]{1,0:T(8,128)} %fusion.59) | copy-start | bytes 786436
  63.0 2.9 %copy-start.10 = (pred[256,256]{1,0:T(8,128)(4,1)S(1)}, pred[256,256]{1,0:T(8,128)(4,1)}, u32[]{:S(2)}) copy-start(pred[256,256]{1,0:T(8,128)(4,1)} %get-tuple-element.50) | copy-start | bytes 196612
  63.0 2.9 %copy-start.11 = (f32[32,256]{1,0:T(8,128)S(1)}, f32[32,256]{1,0:T(8,128)}, u32[]{:S(2)}) copy-start(f32[32,256]{1,0:T(8,128)} %get-tuple-element.24) | copy-start | bytes 98308
  63.0 2.9 %copy-start.13 = (f32[32,256]{1,0:T(8,128)S(1)}, f32[32,256]{1,0:T(8,128)}, u32[]{:S(2)}) copy-start(f32[32,256]{1,0:T(8,128)} %fusion.81) | copy-start | bytes 98308
  63.0 2.9 %copy-start.20 = (pred[256]{0:T(512)(128)(4,1)S(1)}, pred[256]{0:T(512)(128)(4,1)}, u32[]{:S(2)}) copy-start(pred[256]{0:T(512)(128)(4,1)} %get-tuple-element.32) | copy-start | bytes 772
  64.2 28.3 %collective-permute-start.2 = (f32[32,64,128]{2,1,0:T(8,128)S(1)}, f32[32,64,128]{2,1,0:T(8,128)S(1)}, u32[]{:S(2)}, u32[]{:S(2)}) collective-permute-start(f32[32,64,128]{2,1,0:T(8,128)S(1)} %fusion.43), channel_id=1, source_target_pairs={{0,4},{4,8},{8,12},{12,16},{16,20},{20,24},{24,28},{28,0},{1,5},{5... | collective-permute-start | bytes 3145736 | tf_op jit(solution)/shard_map/while/body/eval_jaxpr/ppermute | solution.py:15
  66.0 10.0 %copy-start.2 = (f32[256,2048]{0,1:T(8,128)S(1)}, f32[256,2048]{0,1:T(8,128)}, u32[]{:S(2)}) copy-start(f32[256,2048]{0,1:T(8,128)} %copy-done.1) | copy-start | bytes 6291460
  66.0 10.0 %copy-start.4 = (f32[32,64,256]{2,1,0:T(8,128)S(1)}, f32[32,64,256]{2,1,0:T(8,128)}, u32[]{:S(2)}) copy-start(f32[32,64,256]{2,1,0:T(8,128)} %fusion.48) | copy-start | bytes 6291460
  66.0 10.0 %copy-start.6 = (f32[256,256]{1,0:T(8,128)S(1)}, f32[256,256]{1,0:T(8,128)}, u32[]{:S(2)}) copy-start(f32[256,256]{1,0:T(8,128)} %fusion.64) | copy-start | bytes 786436
  66.0 10.0 %copy-start.9 = (pred[256,256]{1,0:T(8,128)(4,1)S(1)}, pred[256,256]{1,0:T(8,128)(4,1)}, u32[]{:S(2)}) copy-start(pred[256,256]{1,0:T(8,128)(4,1)} %get-tuple-element.51) | copy-start | bytes 196612
  66.0 10.0 %copy-start.12 = (f32[32,256]{1,0:T(8,128)S(1)}, f32[32,256]{1,0:T(8,128)}, u32[]{:S(2)}) copy-start(f32[32,256]{1,0:T(8,128)} %get-tuple-element.25) | copy-start | bytes 98308
  66.0 10.0 %copy-start.14 = (f32[32,256]{1,0:T(8,128)S(1)}, f32[32,256]{1,0:T(8,128)}, u32[]{:S(2)}) copy-start(f32[32,256]{1,0:T(8,128)} %fusion.79) | copy-start | bytes 98308
  66.0 10.0 %copy-start.19 = (pred[256]{0:T(512)(128)(4,1)S(1)}, pred[256]{0:T(512)(128)(4,1)}, u32[]{:S(2)}) copy-start(pred[256]{0:T(512)(128)(4,1)} %get-tuple-element.34) | copy-start | bytes 772
  76.1 16.5 %copy-start = (f32[512,2048]{0,1:T(8,128)S(1)}, f32[512,2048]{0,1:T(8,128)}, u32[]{:S(2)}) copy-start(f32[512,2048]{0,1:T(8,128)} %copy.68) | copy-start | bytes 12582916
  76.1 16.5 %copy-start.16 = (pred[512]{0:T(512)(128)(4,1)S(1)}, pred[512]{0:T(512)(128)(4,1)}, u32[]{:S(2)}) copy-start(pred[512]{0:T(512)(128)(4,1)} %get-tuple-element.11) | copy-start | bytes 1540
where the time goes:
time: 98.6 us; the launch traced here: 98 us
  matrix products  32 us (32%)
  other arithmetic  27.6 us (28%)
  local copies, waits for them, and re-layouts  17.1 us (17%)
  starting transfers between devices  6.29 us (6%)
  waiting for transfers between devices  6.22 us (6%)
  blocking collectives  5.79 us (6%)
  between operations  2.89 us (3%)
    dot_general x2, matrix products, block_pass(): output = jnp.einsum('hts,shp->htp', weights, values, precision=high)  20.2 us
    ppermute x3, starting transfers between devices, shifted(): return lax.ppermute(value, axis, pairs)  6.29 us
    ppermute x3, waiting for transfers between devices, shifted(): return lax.ppermute(value, axis, pairs)  6.22 us
    slice x3, local copies, waits for them, and re-layouts, on_device(): block_values = x_conv[low:high_end].reshape(BLOCK, local_heads, HDIM)  6.14 us
    another operation x12, other arithmetic  5.84 us
    all_gather x1, blocking collectives, on_device(): lax.all_gather(bc_local, 'head', axis=1, tiled=True).astype(jnp.float32)  5.79 us
    mul x1, local copies, waits for them, and re-layouts, gated_norm(): jax.nn.silu(gate.astype(jnp.float32)).reshape(rows, heads, width)  5.5 us
    dot_general x2, matrix products, block_pass(): carried = jnp.einsum('tn,hpn->htp', cmat, state, precision=high)  4.66 us
  transfers between devices with their start and end apart: 3, of which 1 were waited for; matrix products, arithmetic and copies ran while one was open for 53% of the time, Pallas kernels for 0%

commit v1 on v0

--- a/solution.py
+++ b/solution.py
@@ -2,11 +2,25 @@
 import jax.numpy as jnp
 from jax import lax
 from jax.sharding import PartitionSpec as P
+from jax.lax import axis_index, axis_size, ppermute
 
 HDIM = 64
 DSTATE = 128
 BLOCK = 256
 CONV = 4
+
+
+def build_paths_over_axis(in_array):
+    total_devices = axis_size("head")
+    seen = tuple(((s, (s + 1) % total_devices) for s in range(total_devices)))
+    steps_seen = tuple(((s, (s - 1) % total_devices) for s in range(total_devices)))
+    side_arr, shaped = ([in_array], [in_array])
+    for _ in range(total_devices // 2):
+        side_arr.append(ppermute(side_arr[-1], "head", seen))
+    for _ in range((total_devices - 1) // 2):
+        shaped.append(ppermute(shaped[-1], "head", steps_seen))
+    back = jnp.concatenate([*side_arr[::-1], *shaped[1:]], axis=1)
+    return jnp.roll(back, (axis_index("head") - total_devices // 2) * in_array.shape[1], 1)
 
 
 def shifted(value, axis, steps):
@@ -73,7 +87,7 @@
     same = jnp.stack([ids_pad[offset : offset + positions] == doc_ids for offset in range(CONV)])
     x_conv = causal_conv(x_pad, conv_x, same)
     bc_local = causal_conv(bc_pad, conv_bc, same).astype(jnp.bfloat16)
-    bc_whole = lax.all_gather(bc_local, "head", axis=1, tiled=True).astype(jnp.float32)
+    bc_whole = build_paths_over_axis(bc_local).astype(jnp.float32)
     bmat = bc_whole[:, :DSTATE]
     cmat = bc_whole[:, DSTATE:]
     blocks = positions // BLOCK

time: 98.6 us -> 86.3 us (0.88)
  blocking collectives: 5.79 us -> 0 us
  other arithmetic: 27.6 us -> 23.9 us
  matrix products: 32 us -> 29.3 us
  waiting for transfers between devices: 6.22 us -> 3.74 us
  starting transfers between devices: 6.29 us -> 8.14 us
    all_gather x1 -> x0, blocking collectives: 5.79 us -> none  [on_device(): lax.all_gather(bc_local, 'head', axis=1, tiled=True).astype(jnp.float32)]
    dot_general x2, matrix products: 4.66 us -> 2.15 us  [block_pass(): carried = jnp.einsum('tn,hpn->htp', cmat, state, precision=high)]
    ppermute x3, waiting for transfers between devices: 6.22 us -> 3.73 us  [shifted(): return lax.ppermute(value, axis, pairs)]
    ppermute x0 -> x3, starting transfers between devices: none -> 1.85 us  [the longest x1 1.73 us: build_paths_over_axis(): shaped.append(ppermute(shaped[-1], 'head', steps_seen))]
    dot_general x2, matrix products: 1.85 us -> 0.54 us  [block_pass(): scores = jnp.dot(cmat, bmat.T, precision=high)]
    another operation x12, other arithmetic: 5.84 us -> 4.61 us
    exp x2, other arithmetic: 1.37 us -> 0.19 us  [block_pass(): jnp.exp(decay_t)[:, :, None] * carried]
  transfers between devices with their start and end apart: 3 -> 6, of which waited for: 1 -> 1; matrix products, arithmetic and copies ran while one was open for 53% -> 67% of each run, Pallas kernels for 0% -> 0%
where the time goes in v1:
time: 86.3 us; the launch traced here: 85.7 us
  matrix products  29.3 us (34%)
  other arithmetic  23.9 us (28%)
  local copies, waits for them, and re-layouts  17.8 us (21%)
  starting transfers between devices  8.14 us (9%)
  waiting for transfers between devices  3.74 us (4%)
  between operations  2.85 us (3%)
    dot_general x2, matrix products, block_pass(): output = jnp.einsum('hts,shp->htp', weights, values, precision=high)  20.1 us
    ppermute x3, starting transfers between devices, shifted(): return lax.ppermute(value, axis, pairs)  6.3 us
    mul x1, local copies, waits for them, and re-layouts, gated_norm(): jax.nn.silu(gate.astype(jnp.float32)).reshape(rows, heads, width)  5.5 us
    slice x3, local copies, waits for them, and re-layouts, on_device(): block_values = x_conv[low:high_end].reshape(BLOCK, local_heads, HDIM)  5.48 us
    mul x1, other arithmetic, gated_norm(): jax.nn.silu(gate.astype(jnp.float32)).reshape(rows, heads, width)  4.66 us
    another operation x12, other arithmetic  4.61 us
    mul x1, other arithmetic, causal_conv(): return jax.nn.silu(total)  4.17 us
    dot_general x2, matrix products, block_pass(): fresh = jnp.einsum('sh,shp,sn->hpn', to_end, values, bmat, precision=high)  3.79 us
  transfers between devices with their start and end apart: 6, of which 1 were waited for; matrix products, arithmetic and copies ran while one was open for 67% of the time, Pallas kernels for 0%

profile of v1, /device:TPU:0, one launch (start us, length us, event | category | flops | bytes accessed | tf_op | source)
XLA Modules:
  0.0 85.7 jit_solution(3680445581704680923)
XLA Ops:
  0.0 1.0 %reduce-window.29 = s32[4,128]{1,0:T(4,128)S(1)} reduce-window(s32[4,128]{1,0:T(4,128)} %bitcast.142, s32[]{:T(128)} %constant.37.clone.1), window={size=1x128 pad=0_0x127_0}, to_apply=%region_0.0 | reduce-window | flops 65024 | bytes 4100 | tf_op jit(solution)/shard_map/reduce-window
  1.8 0.6 fusion.80
  2.4 0.7 slice_compare_fusion
  3.1 1.0 %copy.44 = bf16[512,64]{1,0:T(8,128)(2,1)S(1)} copy(bf16[512,64]{0,1:T(8,128)(2,1)} %param.11) | data formatting | bytes 131072 | tf_op args[2]
  4.1 3.0 %collective-permute-start = (bf16[3,64]{1,0:T(4,128)(2,1)S(1)}, bf16[3,64]{1,0:T(4,128)(2,1)S(1)}, u32[]{:S(2)}, u32[]{:S(2)}) collective-permute-start(bf16[3,64]{1,0:T(4,128)(2,1)S(1)} %slice_select_fusion.1), channel_id=1, source_target_pairs={{0,4},{4,8},{8,12},{12,16},{16,20},{20,24},{24,28},{28,0},{1,5},{5... | collective-permute-start | bytes 1160 | tf_op jit(solution)/shard_map/ppermute | solution.py:29
  7.1 0.8 slice_select_fusion
  7.9 1.6 %collective-permute-start.4 = (bf16[3,2048]{1,0:T(4,128)(2,1)S(1)}, bf16[3,2048]{1,0:T(4,128)(2,1)S(1)}, u32[]{:S(2)}, u32[]{:S(2)}) collective-permute-start(bf16[3,2048]{1,0:T(4,128)(2,1)S(1)} %slice_select_fusion), channel_id=1, source_target_pairs={{0,4},{4,8},{8,12},{12,16},{16,20},{20,24},{24,28},{28,0},{1,5},{5... | collective-permute-start | bytes 36872 | tf_op jit(solution)/shard_map/ppermute | solution.py:29
  9.6 0.7 slice.189
  11.0 0.8 multiply_bitcast_fusion.2
  13.5 0.9 %copy_bitcast_fusion = f32[32,4,128]{2,0,1:T(8,128)S(1)} fusion(f32[512,32]{0,1:T(8,128)} %param.12, f32[32]{0:T(128)} %param.13), kind=kLoop, calls=%fused_computation.61 | loop fusion | flops 32768 | bytes 131200 | tf_op jit(solution)/shard_map/reshape.13
  15.3 1.2 %reduce-window.39 = f32[32,4,128]{2,0,1:T(8,128)S(1)} reduce-window(f32[32,4,128]{2,0,1:T(8,128)S(1)} %copy_bitcast_fusion, f32[]{:T(128)} %constant.39.clone.1), window={size=1x1x128 pad=0_0x0_0x127_0}, to_apply=%region_6.7 | reduce-window | flops 2080768 | bytes 131076 | tf_op jit(solution)/shard_map/reduce-window.6
  16.9 0.8 bitcast_convert_fusion.3
  17.7 0.9 %slice_convert_fusion.3 = (f32[1,2048]{1,0:T(1,128)S(1)}, f32[1,2048]{1,0:T(1,128)S(1)}, f32[1,2048]{1,0:T(1,128)S(1)}, f32[1,2048]{1,0:T(1,128)S(1)}) fusion(bf16[4,2048]{1,0:T(4,128)(2,1)} %param.14), kind=kLoop, calls=%fused_computation.102 | loop fusion | flops 8192 | bytes 49152 | tf_op jit(solution)/shard_map/mul | solution.py:36
  19.8 2.4 %broadcast_compare_fusion.1 = (pred[256]{0:T(512)(128)(4,1)S(1)}, pred[256]{0:T(512)(128)(4,1)}, pred[256]{0:T(512)(128)(4,1)S(1)}, pred[256]{0:T(512)(128)(4,1)}) fusion(s32[]{:T(128)} %bitcast.27, s32[4,128]{1,0:T(4,128)S(1)} %get-tuple-element.16, s32[]{:T(128)} %bitcast.19, s32[]{:T(128)} %bitcast.20), kind=kLoop, calls=%fused_computation.126 | loop fusion | flops 1024 | bytes 3084 | tf_op jit(solution)/shard_map/eq | solution.py:59
  24.5 4.7 %convert_multiply_fusion = f32[512,2048]{1,0:T(8,128)} fusion(bf16[512,2048]{1,0:T(8,128)(2,1)} %param.10), kind=kLoop, calls=%fused_computation.12 | loop fusion | flops 5242880 | bytes 6291456 | tf_op jit(solution)/shard_map/jit(silu)/mul | solution.py:68
  29.2 0.8 fusion.63
  30.0 5.5 %copy.53 = f32[512,2048]{0,1:T(8,128)} copy(f32[512,2048]{1,0:T(8,128)} %convert_multiply_fusion) | data formatting | bytes 8388608 | tf_op jit(solution)/shard_map/jit(silu)/mul | solution.py:68
  35.9 1.7 %collective-permute-start.3 = (bf16[512,64]{1,0:T(8,128)(2,1)S(1)}, bf16[512,64]{1,0:T(8,128)(2,1)S(1)}, u32[]{:S(2)}, u32[]{:S(2)}) collective-permute-start(bf16[512,64]{1,0:T(8,128)(2,1)S(1)} %multiply_convert_fusion.1), channel_id=1, source_target_pairs={{0,3},{1,0},{2,1},{3,2},{4,7},{5,4},{6,5},{7,6},{8,11},{9,8},{10,9... | collective-permute-start | bytes 196616 | tf_op jit(solution)/shard_map/ppermute | solution.py:21
  37.7 4.2 %divide_multiply_fusion = f32[512,2048]{1,0:T(8,128)S(1)} fusion(bf16[512,2048]{1,0:T(8,128)(2,1)S(1)} %copy-done.2, bf16[3,2048]{1,0:T(4,128)(2,1)S(1)} %collective-permute-done.4, f32[2048]{0:T(1024)S(1)} %bitcast.140, f32[2048]{0:T(1024)S(1)} %bitcast.141, f32[2048]{0:T(1024)S(1)} %bitcast.139, f32[2048]{0:T(1024)S(1)} %bitcast.138, ...), kind=kLoop, calls=%fused_computation.25 | loop fusion | flops 28311552 | bytes 6338048 | tf_op jit(solution)/shard_map/jit(silu)/mul | solution.py:40
  41.9 1.7 %fusion.79 = (f32[256,2048]{1,0:T(8,128)}, f32[256,2048]{1,0:T(8,128)S(1)}) fusion(f32[512,2048]{1,0:T(8,128)S(1)} %divide_multiply_fusion), kind=kLoop, calls=%fused_computation.138 | loop fusion | bytes 8388608 | tf_op jit(solution)/shard_map/slice | solution.py:101
  43.6 1.9 %copy.50 = f32[256,2048]{0,1:T(8,128)} copy(f32[256,2048]{1,0:T(8,128)S(1)} %get-tuple-element.20) | data formatting | bytes 4194304 | tf_op jit(solution)/shard_map/slice | solution.py:101
  45.5 1.9 %copy.47 = f32[256,2048]{0,1:T(8,128)S(1)} copy(f32[256,2048]{1,0:T(8,128)} %get-tuple-element.18) | data formatting | bytes 4194304 | tf_op jit(solution)/shard_map/slice | solution.py:101
  47.9 1.9 %fusion.33 = f32[32,64,128]{2,1,0:T(8,128)S(1)} fusion(f32[256,32,64]{0,2,1:T(8,128)S(1)} %bitcast.131, f32[256,32]{0,1:T(8,128)S(1)} %exponential_select_fusion.1, f32[32]{0:T(128)} %fusion.71, bf16[512,512]{1,0:T(8,128)(2,1)S(1)} %concatenate.20, s32[]{:T(128)S(6)} %select_n.116), kind=kOutput, calls=%fused_computation.44 | convolution fusion | flops 806092800 | bytes 3244164 | tf_op jit(solution)/shard_map/sh,shp,sn->hpn/dot_general | solution.py:61
  49.8 1.9 %add_add_fusion = f32[32,64,128]{2,1,0:T(8,128)S(1)} fusion(f32[32,64,128]{2,1,0:T(8,128)S(1)} %fusion.33, f32[32]{0:T(128)} %broadcast_select_fusion, f32[32]{0:T(128)} %fusion.63, f32[256,32,64]{0,2,1:T(8,128)S(1)} %bitcast.133, f32[256,32]{0,1:T(8,128)S(1)} %exponential_select_fusion, bf16[512,512]{1,0:T(8,128)(2,1)S(1)} %concatenate.20, s32[]{:T(128)S(6)} %add.101, ...), kind=kOutput, calls=%fused_computation.45 | convolution fusion | flops 806617088 | bytes 4292872 | tf_op jit(solution)/shard_map/sh,shp,sn->hpn/dot_general | solution.py:61
  51.7 1.8 %collective-permute-start.5 = (f32[32,64,128]{2,1,0:T(8,128)S(1)}, f32[32,64,128]{2,1,0:T(8,128)S(1)}, u32[]{:S(2)}, u32[]{:S(2)}) collective-permute-start(f32[32,64,128]{2,1,0:T(8,128)S(1)} %add_add_fusion), channel_id=1, source_target_pairs={{0,4},{4,8},{8,12},{12,16},{16,20},{20,24},{24,28},{28,0},{1,5},{5... | collective-permute-start | bytes 3145736 | tf_op jit(solution)/shard_map/while/body/eval_jaxpr/ppermute | solution.py:29
  53.8 9.9 %fusion.6 = f32[32,256,64]{1,2,0:T(8,128)S(1)} fusion(f32[256,32,64]{0,2,1:T(8,128)S(1)} %bitcast.132, f32[256,256]{1,0:T(8,128)S(1)} %fusion.52, f32[32,256]{1,0:T(8,128)S(1)} %get-tuple-element.25, pred[256,256]{1,0:T(8,128)(4,1)S(1)} %get-tuple-element.51), kind=kOutput, calls=%fused_computation.6 | convolution fusion | flops 1619001344 | bytes 4554752 | tf_op jit(solution)/shard_map/hts,shp->htp/dot_general | solution.py:55
  63.7 1.1 %bitcast_add_fusion.1 = f32[32,256,64]{1,2,0:T(8,128)S(1)} fusion(f32[32,256,64]{1,2,0:T(8,128)S(1)} %fusion.6, f32[32,256]{1,0:T(8,128)S(1)} %fusion.75, pred[256]{0:T(512)(128)(4,1)S(1)} %copy-done.6, bf16[512,512]{1,0:T(8,128)(2,1)S(1)} %concatenate.20, s32[]{:T(128)S(6)} %add.100), kind=kOutput, calls=%fused_computation.39 | convolution fusion | flops 806879232 | bytes 4293124 | tf_op jit(solution)/shard_map/tn,hpn->htp/dot_general | solution.py:57
  65.1 10.2 %fusion = f32[32,256,64]{1,2,0:T(8,128)S(1)} fusion(f32[256,32,64]{0,2,1:T(8,128)S(1)} %bitcast.134, f32[256,256]{1,0:T(8,128)S(1)} %fusion.57, f32[32,256]{1,0:T(8,128)S(1)} %get-tuple-element.24, pred[256,256]{1,0:T(8,128)(4,1)S(1)} %get-tuple-element.50), kind=kOutput, calls=%fused_computation | convolution fusion | flops 1619001344 | bytes 4554752 | tf_op jit(solution)/shard_map/hts,shp->htp/dot_general | solution.py:55
  75.3 1.1 %bitcast_add_fusion = f32[32,256,64]{1,2,0:T(8,128)S(1)} fusion(f32[32,256,64]{1,2,0:T(8,128)S(1)} %fusion, f32[32,64,128]{2,1,0:T(8,128)S(1)} %fusion.33, f32[32,256]{1,0:T(8,128)S(1)} %fusion.77, pred[256]{0:T(512)(128)(4,1)S(1)} %copy-done.5, bf16[512,512]{1,0:T(8,128)(2,1)S(1)} %concatenate.20, s32[]{:T(128)S(6)} %add.101, s32[]{:T(128)S(6)} %add.100), kind=kOutput, calls=%fused_computation.38 | convolution fusion | flops 806879232 | bytes 5341704 | tf_op jit(solution)/shard_map/tn,hpn->htp/dot_general | solution.py:57
  76.4 3.7 %collective-permute-done.5 = f32[32,64,128]{2,1,0:T(8,128)S(1)} collective-permute-done((f32[32,64,128]{2,1,0:T(8,128)S(1)}, f32[32,64,128]{2,1,0:T(8,128)S(1)}, u32[]{:S(2)}, u32[]{:S(2)}) %collective-permute-start.5) | collective-permute-done | bytes 1048608 | tf_op jit(solution)/shard_map/while/body/eval_jaxpr/ppermute | solution.py:29
  80.1 2.6 %multiply_reduce_fusion = (f32[512,32]{0,1:T(8,128)S(1)}, f32[512,32,64]{0,2,1:T(8,128)S(1)}) fusion(f32[512,32,64]{0,2,1:T(8,128)S(1)} %bitcast.129, f32[32,64,128]{2,1,0:T(8,128)S(1)} %collective-permute-done.5, bf16[512,512]{1,0:T(8,128)(2,1)S(1)} %concatenate.20, s32[]{:T(128)S(6)} %add.100, f32[32,512]{1,0:T(8,128)S(1)} %bitcast_exponential_fusion, ...), kind=kOutput, calls=%fused_computation.21 | convolution fusion | flops 1617936384 | bytes 13894148 | tf_op jit(solution)/shard_map/tn,hpn->htp/dot_general | solution.py:121
  83.3 2.4 %copy.54 = bf16[512,2048]{1,0:T(8,128)(2,1)} copy(bf16[512,2048]{0,1:T(8,128)(2,1)S(1)} %bitcast.130) | data formatting | bytes 4194304 | tf_op jit(solution)/shard_map/convert_element_type | solution.py:71
  (61 shorter events, 7.6 us)
Async XLA Ops:
  4.1 31.4 %collective-permute-start = (bf16[3,64]{1,0:T(4,128)(2,1)S(1)}, bf16[3,64]{1,0:T(4,128)(2,1)S(1)}, u32[]{:S(2)}, u32[]{:S(2)}) collective-permute-start(bf16[3,64]{1,0:T(4,128)(2,1)S(1)} %slice_select_fusion.1), channel_id=1, source_target_pairs={{0,4},{4,8},{8,12},{12,16},{16,20},{20,24},{24,28},{28,0},{1,5},{5... | collective-permute-start | bytes 1160 | tf_op jit(solution)/shard_map/ppermute | solution.py:29
  7.9 29.7 %collective-permute-start.4 = (bf16[3,2048]{1,0:T(4,128)(2,1)S(1)}, bf16[3,2048]{1,0:T(4,128)(2,1)S(1)}, u32[]{:S(2)}, u32[]{:S(2)}) collective-permute-start(bf16[3,2048]{1,0:T(4,128)(2,1)S(1)} %slice_select_fusion), channel_id=1, source_target_pairs={{0,4},{4,8},{8,12},{12,16},{16,20},{20,24},{24,28},{28,0},{1,5},{5... | collective-permute-start | bytes 36872 | tf_op jit(solution)/shard_map/ppermute | solution.py:29
  30.0 5.5 %copy-start.3 = (bf16[2048]{0:T(1024)(128)(2,1)S(1)}, bf16[2048]{0:T(1024)(128)(2,1)}, u32[]{:S(2)}) copy-start(bf16[2048]{0:T(1024)(128)(2,1)} %param.16) | copy-start | bytes 12292
  30.0 7.7 %copy-start.2 = (bf16[512,2048]{1,0:T(8,128)(2,1)S(1)}, bf16[512,2048]{1,0:T(8,128)(2,1)}, u32[]{:S(2)}) copy-start(bf16[512,2048]{1,0:T(8,128)(2,1)} %param.9) | copy-start | bytes 6291460
  35.9 6.0 %collective-permute-start.1 = (bf16[512,64]{1,0:T(8,128)(2,1)S(1)}, bf16[512,64]{1,0:T(8,128)(2,1)S(1)}, u32[]{:S(2)}, u32[]{:S(2)}) collective-permute-start(bf16[512,64]{1,0:T(8,128)(2,1)S(1)} %multiply_convert_fusion.1), channel_id=1, source_target_pairs={{0,1},{1,2},{2,3},{3,0},{4,5},{5,6},{6,7},{7,4},{8,9},{9,10},{10,1... | collective-permute-start | bytes 196616 | tf_op jit(solution)/shard_map/ppermute | solution.py:19
  35.9 11.5 %collective-permute-start.3 = (bf16[512,64]{1,0:T(8,128)(2,1)S(1)}, bf16[512,64]{1,0:T(8,128)(2,1)S(1)}, u32[]{:S(2)}, u32[]{:S(2)}) collective-permute-start(bf16[512,64]{1,0:T(8,128)(2,1)S(1)} %multiply_convert_fusion.1), channel_id=1, source_target_pairs={{0,3},{1,0},{2,1},{3,2},{4,7},{5,4},{6,5},{7,6},{8,11},{9,8},{10,9... | collective-permute-start | bytes 196616 | tf_op jit(solution)/shard_map/ppermute | solution.py:21
  41.9 5.6 %collective-permute-start.2 = (bf16[512,64]{1,0:T(8,128)(2,1)S(1)}, bf16[512,64]{1,0:T(8,128)(2,1)S(1)}, u32[]{:S(2)}, u32[]{:S(2)}) collective-permute-start(bf16[512,64]{1,0:T(8,128)(2,1)S(1)} %collective-permute-done.1), channel_id=1, source_target_pairs={{0,1},{1,2},{2,3},{3,0},{4,5},{5,6},{6,7},{7,4},{8,9},{9,10},{10,1... | collective-permute-start | bytes 196616 | tf_op jit(solution)/shard_map/ppermute | solution.py:19
  47.9 1.9 %copy-start.1 = (f32[256,2048]{0,1:T(8,128)S(1)}, f32[256,2048]{0,1:T(8,128)}, u32[]{:S(2)}) copy-start(f32[256,2048]{0,1:T(8,128)} %copy.50) | copy-start | bytes 6291460
  51.7 28.4 %collective-permute-start.5 = (f32[32,64,128]{2,1,0:T(8,128)S(1)}, f32[32,64,128]{2,1,0:T(8,128)S(1)}, u32[]{:S(2)}, u32[]{:S(2)}) collective-permute-start(f32[32,64,128]{2,1,0:T(8,128)S(1)} %add_add_fusion), channel_id=1, source_target_pairs={{0,4},{4,8},{8,12},{12,16},{16,20},{20,24},{24,28},{28,0},{1,5},{5... | collective-permute-start | bytes 3145736 | tf_op jit(solution)/shard_map/while/body/eval_jaxpr/ppermute | solution.py:29
  53.8 9.9 %copy-start.6 = (pred[256]{0:T(512)(128)(4,1)S(1)}, pred[256]{0:T(512)(128)(4,1)}, u32[]{:S(2)}) copy-start(pred[256]{0:T(512)(128)(4,1)} %get-tuple-element.34) | copy-start | bytes 772
  65.1 10.2 %copy-start.5 = (pred[256]{0:T(512)(128)(4,1)S(1)}, pred[256]{0:T(512)(128)(4,1)}, u32[]{:S(2)}) copy-start(pred[256]{0:T(512)(128)(4,1)} %get-tuple-element.32) | copy-start | bytes 772
  75.3 4.8 %copy-start = (f32[512,2048]{0,1:T(8,128)S(1)}, f32[512,2048]{0,1:T(8,128)}, u32[]{:S(2)}) copy-start(f32[512,2048]{0,1:T(8,128)} %copy.53) | copy-start | bytes 12582916
  75.3 4.8 %copy-start.4 = (pred[512]{0:T(512)(128)(4,1)S(1)}, pred[512]{0:T(512)(128)(4,1)}, u32[]{:S(2)}) copy-start(pred[512]{0:T(512)(128)(4,1)} %get-tuple-element.11) | copy-start | bytes 1540
